TPU v7x, 32 devices: a whole 2x2x4 slice. The times are simulated.
32 devices in a mesh: row: 4 (over z), col: 8 (over y, x, core).
Axes of the slice: x: 2, y: 2, z: 4, core: 2. Of those that a mesh axis runs over, the one named last changes fastest.
Arguments:
- gram: bfloat16 [2, 4, 256, 16, 8, 256], P(None, 'row', None, None, 'col'), as said below
Outputs:
- schur: float32 [2, 4, 256, 16, 8, 256], P(None, 'row', None, None, 'col')
Inputs may be any that keep to these rules, and one draw needn't show every extreme that they name: `gram`: the first 2048 columns of the slab form a symmetric matrix, and its leading 2 * 256 x 2 * 256 block is positive definite with smallest eigenvalue above 10.
All inputs are finite; a program needn't handle non-finite values.
Results may differ from a plain program's by a relative error of at most 0.0018.
Values may be sent and summed in bfloat16 or wider, within the bound.
No kernel may reach another device: no remote copies, remote signals or barrier semaphores. Data moves between devices by JAX's collectives and lax.ppermute only.
A program may use at most 64 MiB of HBM per device.

v0:
```python
import jax
import jax.numpy as jnp
from jax import lax
from jax.sharding import PartitionSpec as P


def from_root(block, axis, source):
    block = jnp.where(lax.axis_index(axis) == source, block, jnp.zeros_like(block))
    return lax.psum(block, axis)


def local(gram):
    n_row = lax.axis_size("row")
    n_col = lax.axis_size("col")
    my_row = lax.axis_index("row")
    my_col = lax.axis_index("col")
    row_slots = gram.shape[0]
    tile_size = gram.shape[2]
    col_slots = gram.shape[3]
    slabs = [gram[row_slot, 0, :, :, 0, :].astype(jnp.float32) for row_slot in range(row_slots)]
    col_tile = jnp.arange(col_slots) * n_col + my_col
    row_tile = jnp.arange(row_slots) * n_row + my_row
    every_slot = list(range(row_slots))
    for panel_index in range(2):
        panel_rows = slabs[panel_index // n_row]
        corner = from_root(
            panel_rows[:, panel_index // n_col, :].astype(jnp.bfloat16), "col", panel_index % n_col
        ).astype(jnp.float32)
        triangle = jnp.linalg.cholesky(corner)
        solved = jax.scipy.linalg.solve_triangular(
            triangle, panel_rows.reshape(tile_size, col_slots * tile_size), lower=True
        )
        solved = solved.reshape(tile_size, col_slots, tile_size)
        solved = jnp.where((col_tile >= panel_index)[None, :, None], solved, 0.0).astype(
            jnp.bfloat16
        )
        factor_across = from_root(solved, "row", panel_index % n_row)
        factor_transposed = []
        for factor_row_slot in range(row_slots):
            target = factor_row_slot * n_row + my_row
            chosen = lax.dynamic_index_in_dim(factor_across, target // n_col, 1, keepdims=False)
            factor_transposed.append(from_root(chosen, "col", target % n_col))
        updated = list(slabs)
        for apply_row_slot in every_slot:
            product = jnp.einsum(
                "pi,pjq->ijq",
                factor_transposed[apply_row_slot],
                factor_across,
                preferred_element_type=jnp.float32,
            )
            updated[apply_row_slot] = updated[apply_row_slot] - product
        slabs = updated
    blocks = jnp.stack(slabs, axis=0)
    retain = (row_tile >= 2)[:, None, None, None] & (col_tile >= 2)[None, None, :, None]
    result = jnp.where(retain, blocks, 0.0)
    return result[:, None, :, :, None, :]


def solution(mesh):
    in_specs = (P(None, "row", None, None, "col", None),)
    out_specs = P(None, "row", None, None, "col", None)
    return jax.shard_map(local, mesh=mesh, in_specs=in_specs, out_specs=out_specs, check_vma=False)
```

profile of v0, /device:TPU:0, one launch (start us, length us, event | category | flops | bytes accessed | tf_op | source)
XLA Modules:
  0.0 609.0 jit_solution(9396137955365741867)
XLA Ops:
  6.5 4.5 fusion.30
  11.0 3.0 copy.24
  14.8 2.5 bitcast_convert_fusion
  17.3 53.2 %all-reduce.9.cloned.1.call-done = bf16[256,256]{0,1:T(8,128)(2,1)} async-done(((bf16[256,256]{0,1:T(8,128)(2,1)}), bf16[256,256]{0,1:T(8,128)(2,1)}) %all-reduce.9.cloned.1.call-update) | async-done | bytes 131088 | tf_op jit(solution)/shard_map/psum | solution.py:9
  72.5 11.7 %cholesky.130 = f32[128,128]{1,0:T(8,128)S(1)} custom-call(f32[128,128]{1,0:T(8,128)S(1)} %cholesky.194), custom_call_target="Cholesky" | custom-call | tf_op jit(solution)/shard_map/jit(cholesky)/cholesky | solution.py:29
  84.2 9.8 %custom-call.13 = f32[1,128,128]{1,2,0:T(8,128)S(1)} custom-call(f32[1,128,128]{2,1,0:T(8,128)S(1)} %get-tuple-element.59), custom_call_target="InvertDiagBlocksLowerTriangular" | custom-call | tf_op jit(solution)/shard_map/jit(cholesky)/cholesky | solution.py:29
  94.5 11.7 %cholesky.147 = f32[128,128]{1,0:T(8,128)S(1)} custom-call(f32[128,128]{1,0:T(8,128)S(1)} %convolution_subtract_fusion.3), custom_call_target="Cholesky" | custom-call | tf_op jit(solution)/shard_map/jit(cholesky)/cholesky | solution.py:29
  108.2 3.9 while.4
  112.2 19.7 %custom-call.14 = f32[2,128,128]{1,2,0:T(8,128)S(1)} custom-call(f32[2,128,128]{2,1,0:T(8,128)S(1)} %get-tuple-element.21), custom_call_target="InvertDiagBlocksLowerTriangular" | custom-call | tf_op jit(solution)/shard_map/jit(_solve_triangular)/triangular_solve | solution.py:30
  131.9 3.7 fusion.6
  135.5 3.5 convolution_subtract_fusion.1
  142.6 4.1 copy.4
  146.7 3.5 fusion.2
  150.3 86.0 %all-reduce.11.cloned.1.call-done = bf16[256,16,256]{0,2,1:T(8,128)(2,1)} async-done(((bf16[256,16,256]{0,2,1:T(8,128)(2,1)}), bf16[256,16,256]{0,2,1:T(8,128)(2,1)}) %all-reduce.11.cloned.1.call-update) | async-done | bytes 2097168 | tf_op jit(solution)/shard_map/psum | solution.py:9
  238.0 53.2 %all-reduce.13.cloned.1.call-done = bf16[256,256]{0,1:T(8,128)(2,1)} async-done(((bf16[256,256]{0,1:T(8,128)(2,1)}), bf16[256,256]{0,1:T(8,128)(2,1)}) %all-reduce.13.cloned.1.call-update) | async-done | bytes 131088 | tf_op jit(solution)/shard_map/psum | solution.py:9
  291.2 2.4 convert_subtract_fusion.1
  293.6 2.0 copy-done
  296.6 52.2 %all-reduce.15.cloned.1.call-done = bf16[256,256]{0,1:T(8,128)(2,1)} async-done(((bf16[256,256]{0,1:T(8,128)(2,1)}), bf16[256,256]{0,1:T(8,128)(2,1)}) %all-reduce.15.cloned.1.call-update) | async-done | bytes 131088 | tf_op jit(solution)/shard_map/psum | solution.py:9
  350.8 11.7 %cholesky.164 = f32[128,128]{1,0:T(8,128)S(1)} custom-call(f32[128,128]{1,0:T(8,128)S(1)} %cholesky.197), custom_call_target="Cholesky" | custom-call | tf_op jit(solution)/shard_map/jit(cholesky)/cholesky | solution.py:29
  363.2 9.8 %custom-call.15 = f32[1,128,128]{1,2,0:T(8,128)S(1)} custom-call(f32[1,128,128]{2,1,0:T(8,128)S(1)} %get-tuple-element.55), custom_call_target="InvertDiagBlocksLowerTriangular" | custom-call | tf_op jit(solution)/shard_map/jit(cholesky)/cholesky | solution.py:29
  373.6 11.7 %cholesky.181 = f32[128,128]{1,0:T(8,128)S(1)} custom-call(f32[128,128]{1,0:T(8,128)S(1)} %convolution_subtract_fusion.2), custom_call_target="Cholesky" | custom-call | tf_op jit(solution)/shard_map/jit(cholesky)/cholesky | solution.py:29
  387.3 4.3 while.5
  391.6 19.7 %custom-call.16 = f32[2,128,128]{1,2,0:T(8,128)S(1)} custom-call(f32[2,128,128]{2,1,0:T(8,128)S(1)} %get-tuple-element.22), custom_call_target="InvertDiagBlocksLowerTriangular" | custom-call | tf_op jit(solution)/shard_map/jit(_solve_triangular)/triangular_solve | solution.py:30
  411.3 3.7 fusion.4
  415.0 3.5 convolution_subtract_fusion
  422.0 3.3 copy.7
  428.8 3.0 copy.25
  431.9 81.4 %all-reduce.17.cloned.1.call-done = bf16[256,16,256]{0,2,1:T(8,128)(2,1)} async-done(((bf16[256,16,256]{0,2,1:T(8,128)(2,1)}), bf16[256,16,256]{0,2,1:T(8,128)(2,1)}) %all-reduce.17.cloned.1.call-update) | async-done | bytes 2097168 | tf_op jit(solution)/shard_map/psum | solution.py:9
  515.1 55.4 %all-reduce.19.cloned.1.call-done = (bf16[256,256]{0,1:T(8,128)(2,1)}, bf16[256,256]{0,1:T(8,128)(2,1)}, bf16[256,256]{0,1:T(8,128)(2,1)}) async-done(((bf16[256,256]{0,1:T(8,128)(2,1)}, bf16[256,256]{0,1:T(8,128)(2,1)}, bf16[256,256]{0,1:T(8,128)(2,1)}), (bf16[256,256]{0,1:T(8,128)(2,1)}, bf16[256,256]{0,1:T(8,128)(2,1)}, bf16[256,256]{0,1:T(8,128)(2,1)})) %all-reduce.19.cloned.1.call-update) | async-done | bytes 393232 | tf_op jit(solution)/shard_map/psum | solution.py:9
  570.5 3.7 subtract_bitcast_fusion
  577.3 3.9 maximum_select_fusion
  581.1 20.5 %copy.15 = f32[2,1,256,16,1,256]{5,4,3,2,1,0:T(1,128)} copy(f32[2,1,256,16,1,256]{2,5,3,4,1,0:T(8,128)} %maximum_select_fusion) | data formatting | bytes 16777216 | tf_op jit(solution)/shard_map/jit(_where)/select_n | solution.py:55
  (82 shorter events, 33.7 us)
Async XLA Ops:
  6.5 64.0 %all-reduce.9.cloned.1.call-start = ((), (), s32[]{:S(2)}) async-start(), calls=%async_computation | async-start | bytes 262144 | tf_op jit(solution)/shard_map/psum | solution.py:9
  14.7 221.5 %all-reduce.11.cloned.1.call-start = ((), (), s32[]{:S(2)}) async-start(), calls=%async_computation.1 | async-start | bytes 4194304 | tf_op jit(solution)/shard_map/psum | solution.py:9
  131.8 3.7 copy-start.2
  150.2 141.0 %all-reduce.13.cloned.1.call-start = ((), (), s32[]{:S(2)}) async-start(), calls=%async_computation.2 | async-start | bytes 262144 | tf_op jit(solution)/shard_map/psum | solution.py:9
  238.0 110.8 %all-reduce.15.cloned.1.call-start = ((), (), s32[]{:S(2)}) async-start(), calls=%async_computation.3 | async-start | bytes 262144 | tf_op jit(solution)/shard_map/psum | solution.py:9
  293.6 2.0 copy-start
  296.3 217.0 %all-reduce.17.cloned.1.call-start = ((), (), s32[]{:S(2)}) async-start(), calls=%async_computation.4 | async-start | bytes 4194304 | tf_op jit(solution)/shard_map/psum | solution.py:9
  411.3 3.7 copy-start.1
  427.2 1.6 copy-start.6
  427.3 143.2 %all-reduce.19.cloned.1.call-start = ((), (), s32[]{:S(2)}) async-start(), calls=%async_computation.5 | async-start | bytes 786432 | tf_op jit(solution)/shard_map/psum | solution.py:9
  570.5 3.8 copy-start.3
  570.5 3.8 copy-start.8
  574.3 1.6 copy-start.4
  574.3 2.2 copy-start.5
  574.3 2.2 copy-start.7
Sparse Core Ops, SparseCore 0:
  14.9 55.6 all-reduce.8
  150.3 85.8 all-reduce.10
  239.3 51.8 all-reduce.12
  296.4 52.3 all-reduce.14
  427.4 85.8 all-reduce.16
  516.9 53.5 all-reduce.18
where the time goes:
time: 618 us; the launch traced here: 609 us
  waiting for transfers between devices  382 us (62%)
  other arithmetic  130 us (21%)
  local copies, waits for them, and re-layouts  53.3 us (9%)
  matrix products  26.9 us (4%)
  between operations  16.8 us (3%)
    psum x6, waiting for transfers between devices, from_root(): return lax.psum(block, axis)  381 us
    another operation x13, other arithmetic, local(): triangle = jnp.linalg.cholesky(corner)  68.6 us
    another operation x7, other arithmetic, local(): jax.scipy.linalg.solve_triangular(triangle, panel_rows.reshape(tile_size,...  42.5 us
    select_n x1, local copies, waits for them, and re-layouts, local(): result = jnp.where(retain, blocks, 0.0)  20.5 us
    another operation x6, matrix products, local(): jax.scipy.linalg.solve_triangular(triangle, panel_rows.reshape(tile_size,...  18.3 us
    another operation x17, local copies, waits for them, and re-layouts, local(): jax.scipy.linalg.solve_triangular(triangle, panel_rows.reshape(tile_size,...  15.2 us
  transfers between devices with their start and end apart: 6, of which 6 were waited for; matrix products, arithmetic and copies ran while one was open for 1% of the time, Pallas kernels for 0%

commit v1 on v0

--- a/solution.py
+++ b/solution.py
@@ -6,7 +6,7 @@
 
 def from_root(block, axis, source):
     block = jnp.where(lax.axis_index(axis) == source, block, jnp.zeros_like(block))
-    return lax.psum(block, axis)
+    return jnp.sum(lax.all_gather(block, axis), axis=0)
 
 
 def local(gram):

time: 618 us -> 676 us (1.094)
  waiting for transfers between devices: 382 us -> 417 us
  other arithmetic: 130 us -> 140 us
    all_gather x0 -> x8, waiting for transfers between devices: none -> 416 us  [from_root(): return jnp.sum(lax.all_gather(block, axis), axis=0)]
    psum x6 -> x0, waiting for transfers between devices: 381 us -> none  [from_root(): return lax.psum(block, axis)]
    reduce_sum x0 -> x8, other arithmetic: none -> 17.4 us  [from_root(): return jnp.sum(lax.all_gather(block, axis), axis=0)]
    unnamed x20 -> x30, local copies, waits for them, and re-layouts: 11 us -> 20.5 us
    another operation x17 -> x15, local copies, waits for them, and re-layouts: 15.2 us -> 8.39 us  [local(): jax.scipy.linalg.solve_triangular(triangle, panel_rows.reshape(tile_size,...]
  transfers between devices with their start and end apart: 6 -> 8, of which waited for: 6 -> 8; matrix products, arithmetic and copies ran while one was open for 1% -> 4% of each run, Pallas kernels for 0% -> 0%
where the time goes in v1:
time: 676 us; the launch traced here: 666 us
  waiting for transfers between devices  417 us (62%)
  other arithmetic  140 us (21%)
  local copies, waits for them, and re-layouts  57.7 us (9%)
  matrix products  32.1 us (5%)
  between operations  17.2 us (3%)
    all_gather x8, waiting for transfers between devices, from_root(): return jnp.sum(lax.all_gather(block, axis), axis=0)  416 us
    another operation x13, other arithmetic, local(): triangle = jnp.linalg.cholesky(corner)  68.8 us
    another operation x7, other arithmetic, local(): jax.scipy.linalg.solve_triangular(triangle, panel_rows.reshape(tile_size,...  40 us
    select_n x1, local copies, waits for them, and re-layouts, local(): result = jnp.where(retain, blocks, 0.0)  20.5 us
    unnamed x30, local copies, waits for them, and re-layouts  20.5 us
    another operation x6, matrix products, local(): jax.scipy.linalg.solve_triangular(triangle, panel_rows.reshape(tile_size,...  18.3 us
    reduce_sum x8, other arithmetic, from_root(): return jnp.sum(lax.all_gather(block, axis), axis=0)  17.4 us
  transfers between devices with their start and end apart: 8, of which 8 were waited for; matrix products, arithmetic and copies ran while one was open for 4% of the time, Pallas kernels for 0%

profile of v1, /device:TPU:0, one launch (start us, length us, event | category | flops | bytes accessed | tf_op | source)
XLA Modules:
  0.0 665.6 jit_solution(6719319239038634329)
XLA Ops:
  6.5 4.5 fusion.32
  11.0 3.0 copy.35
  17.3 23.9 %all-gather.19.cloned.1.call-done = bf16[2048,1,256]{0,2,1:T(8,128)(2,1)} async-done(((bf16[256,1,256]{0,2,1:T(8,128)(2,1)}), bf16[2048,1,256]{0,2,1:T(8,128)(2,1)}) %all-gather.19.cloned.1.call-update) | async-done | bytes 1048592 | tf_op jit(solution)/shard_map/all_gather | solution.py:9
  43.7 11.7 %cholesky.130 = f32[128,128]{1,0:T(8,128)S(1)} custom-call(f32[128,128]{1,0:T(8,128)S(1)} %cholesky.194), custom_call_target="Cholesky" | custom-call | tf_op jit(solution)/shard_map/jit(cholesky)/cholesky | solution.py:29
  55.4 9.8 %custom-call.13 = f32[1,128,128]{1,2,0:T(8,128)S(1)} custom-call(f32[1,128,128]{2,1,0:T(8,128)S(1)} %get-tuple-element.56), custom_call_target="InvertDiagBlocksLowerTriangular" | custom-call | tf_op jit(solution)/shard_map/jit(cholesky)/cholesky | solution.py:29
  65.7 11.7 %cholesky.147 = f32[128,128]{1,0:T(8,128)S(1)} custom-call(f32[128,128]{1,0:T(8,128)S(1)} %convolution_subtract_fusion.3), custom_call_target="Cholesky" | custom-call | tf_op jit(solution)/shard_map/jit(cholesky)/cholesky | solution.py:29
  79.6 4.6 while.4
  84.2 19.7 %custom-call.14 = f32[2,128,128]{1,2,0:T(8,128)S(1)} custom-call(f32[2,128,128]{2,1,0:T(8,128)S(1)} %get-tuple-element.21), custom_call_target="InvertDiagBlocksLowerTriangular" | custom-call | tf_op jit(solution)/shard_map/jit(_solve_triangular)/triangular_solve | solution.py:30
  103.9 3.7 fusion.8
  107.6 3.5 convolution_subtract_fusion.1
  116.1 149.7 %all-gather.15.cloned.1.call-done = bf16[4,256,16,256]{3,2,1,0:T(8,128)(2,1)} async-done(((bf16[1,256,16,256]{3,2,1,0:T(8,128)(2,1)}), bf16[4,256,16,256]{3,2,1,0:T(8,128)(2,1)}) %all-gather.15.cloned.1.call-update) | async-done | bytes 8388624 | tf_op jit(solution)/shard_map/all_gather | solution.py:9
  265.8 6.6 reduce_sum.97
  272.4 3.0 copy.15
  276.3 21.9 %all-gather.21.cloned.1.call-done = bf16[2048,1,256]{0,2,1:T(8,128)(2,1)} async-done(((bf16[256,1,256]{0,2,1:T(8,128)(2,1)}), bf16[2048,1,256]{0,2,1:T(8,128)(2,1)}) %all-gather.21.cloned.1.call-update) | async-done | bytes 1048592 | tf_op jit(solution)/shard_map/all_gather | solution.py:9
  304.4 23.5 %all-gather.23.cloned.1.call-done = bf16[2048,1,256]{0,2,1:T(8,128)(2,1)} async-done(((bf16[256,1,256]{0,2,1:T(8,128)(2,1)}), bf16[2048,1,256]{0,2,1:T(8,128)(2,1)}) %all-gather.23.cloned.1.call-update) | async-done | bytes 1048592 | tf_op jit(solution)/shard_map/all_gather | solution.py:9
  330.3 11.7 %cholesky.164 = f32[128,128]{1,0:T(8,128)S(1)} custom-call(f32[128,128]{1,0:T(8,128)S(1)} %cholesky.197), custom_call_target="Cholesky" | custom-call | tf_op jit(solution)/shard_map/jit(cholesky)/cholesky | solution.py:29
  342.1 9.8 %custom-call.15 = f32[1,128,128]{1,2,0:T(8,128)S(1)} custom-call(f32[1,128,128]{2,1,0:T(8,128)S(1)} %get-tuple-element.52), custom_call_target="InvertDiagBlocksLowerTriangular" | custom-call | tf_op jit(solution)/shard_map/jit(cholesky)/cholesky | solution.py:29
  352.4 11.7 %cholesky.181 = f32[128,128]{1,0:T(8,128)S(1)} custom-call(f32[128,128]{1,0:T(8,128)S(1)} %convolution_subtract_fusion.2), custom_call_target="Cholesky" | custom-call | tf_op jit(solution)/shard_map/jit(cholesky)/cholesky | solution.py:29
  367.0 4.4 while.5
  371.4 19.7 %custom-call.16 = f32[2,128,128]{1,2,0:T(8,128)S(1)} custom-call(f32[2,128,128]{2,1,0:T(8,128)S(1)} %get-tuple-element.22), custom_call_target="InvertDiagBlocksLowerTriangular" | custom-call | tf_op jit(solution)/shard_map/jit(_solve_triangular)/triangular_solve | solution.py:30
  391.1 3.7 fusion.6
  394.8 3.5 convolution_subtract_fusion
  404.1 148.9 %all-gather.17.cloned.1.call-done = bf16[4,256,16,256]{3,2,1,0:T(8,128)(2,1)} async-done(((bf16[1,256,16,256]{3,2,1,0:T(8,128)(2,1)}), bf16[4,256,16,256]{3,2,1,0:T(8,128)(2,1)}) %all-gather.17.cloned.1.call-update) | async-done | bytes 8388624 | tf_op jit(solution)/shard_map/all_gather | solution.py:9
  553.0 6.1 reduce_sum.100
  561.4 4.3 copy.37
  565.8 10.7 %all-gather.27.cloned.1.call-done = bf16[2048,1,256]{0,2,1:T(8,128)(2,1)} async-done(((bf16[256,1,256]{0,2,1:T(8,128)(2,1)}), bf16[2048,1,256]{0,2,1:T(8,128)(2,1)}) %all-gather.27.cloned.1.call-update) | async-done | bytes 1048592 | tf_op jit(solution)/shard_map/all_gather | solution.py:9
  581.8 20.3 %all-gather.25.cloned.1.call-done = bf16[2048,1,256]{0,2,1:T(8,128)(2,1)} async-done(((bf16[256,1,256]{0,2,1:T(8,128)(2,1)}), bf16[2048,1,256]{0,2,1:T(8,128)(2,1)}) %all-gather.25.cloned.1.call-update) | async-done | bytes 1048592 | tf_op jit(solution)/shard_map/all_gather | solution.py:9
  604.3 5.5 subtract_bitcast_fusion
  609.9 17.6 %all-gather.29.cloned.1.call-done = bf16[2048,1,256]{0,2,1:T(8,128)(2,1)} async-done(((bf16[256,1,256]{0,2,1:T(8,128)(2,1)}), bf16[2048,1,256]{0,2,1:T(8,128)(2,1)}) %all-gather.29.cloned.1.call-update) | async-done | bytes 1048592 | tf_op jit(solution)/shard_map/all_gather | solution.py:9
  630.0 3.9 fusion.3
  633.9 3.9 maximum_select_fusion
  637.8 20.5 %copy.29 = f32[2,1,256,16,1,256]{5,4,3,2,1,0:T(1,128)} copy(f32[2,1,256,16,1,256]{2,5,3,4,1,0:T(8,128)} %maximum_select_fusion) | data formatting | bytes 16777216 | tf_op jit(solution)/shard_map/jit(_where)/select_n | solution.py:55
  (107 shorter events, 49.7 us)
Async XLA Ops:
  6.5 34.7 %all-gather.19.cloned.1.call-start = ((), (), s32[]{:S(2)}) async-start(), calls=%async_computation.2 | async-start | bytes 1179648 | tf_op jit(solution)/shard_map/all_gather | solution.py:9
  14.0 3.3 copy-start.4
  14.8 251.0 %all-gather.15.cloned.1.call-start = ((), (), s32[]{:S(2)}) async-start(), calls=%async_computation | async-start | bytes 10485760 | tf_op jit(solution)/shard_map/all_gather | solution.py:9
  103.9 3.7 copy-start.6
  116.0 182.2 %all-gather.21.cloned.1.call-start = ((), (), s32[]{:S(2)}) async-start(), calls=%async_computation.3 | async-start | bytes 1179648 | tf_op jit(solution)/shard_map/all_gather | solution.py:9
  275.4 26.0 %copy-start.2 = (bf16[256,16,256]{0,2,1:T(8,128)(2,1)}, bf16[256,16,256]{0,2,1:T(8,128)(2,1)S(1)}, u32[]{:S(2)}) copy-start(bf16[256,16,256]{0,2,1:T(8,128)(2,1)S(1)} %copy.15) | copy-start | bytes 6291460
  276.3 51.6 %all-gather.23.cloned.1.call-start = ((), (), s32[]{:S(2)}) async-start(), calls=%async_computation.4 | async-start | bytes 1179648 | tf_op jit(solution)/shard_map/all_gather | solution.py:9
  298.2 2.5 copy-start.5
  301.5 2.0 copy-start
  304.1 248.8 %all-gather.17.cloned.1.call-start = ((), (), s32[]{:S(2)}) async-start(), calls=%async_computation.1 | async-start | bytes 10485760 | tf_op jit(solution)/shard_map/all_gather | solution.py:9
  391.1 3.7 copy-start.1
  403.2 173.4 %all-gather.27.cloned.1.call-start = ((), (), s32[]{:S(2)}) async-start(), calls=%async_computation.6 | async-start | bytes 1179648 | tf_op jit(solution)/shard_map/all_gather | solution.py:9
  403.8 198.3 %all-gather.25.cloned.1.call-start = ((), (), s32[]{:S(2)}) async-start(), calls=%async_computation.5 | async-start | bytes 1179648 | tf_op jit(solution)/shard_map/all_gather | solution.py:9
  560.5 67.0 %all-gather.29.cloned.1.call-start = ((), (), s32[]{:S(2)}) async-start(), calls=%async_computation.7 | async-start | bytes 1179648 | tf_op jit(solution)/shard_map/all_gather | solution.py:9
  576.6 2.5 copy-start.3
  627.5 2.5 copy-start.8
  630.0 3.9 copy-start.7
Sparse Core Ops, SparseCore 0:
  14.9 26.2 all-gather.18
  116.1 149.6 all-gather.14
  276.4 21.7 all-gather.20
  304.3 23.5 all-gather.22
  403.3 149.6 all-gather.16
  554.7 21.7 all-gather.26
  578.4 23.5 all-gather.24
  603.9 23.5 all-gather.28
